TPU v7x, 32 devices: a whole 2x2x4 slice. The times are simulated.
32 devices in a mesh: cells: 8 (over z, x), genes: 4 (over y, core).
Axes of the slice: x: 2, y: 2, z: 4, core: 2. Of those that a mesh axis runs over, the one named last changes fastest.
Arguments:
- counts: bfloat16 [8192, 13500], P('cells', 'genes'), may hold values from 0.0099487305 to 200
- library: int32 [8192], P('cells'), may hold values from 1000 to 20000
- cell_mask: int32 [8192], P('cells'), may hold values 0 or 1
- slide_len: int32 [3], replicated, may hold values from 1 to 4096, 8192 in all
- kl_step: int32 [1], replicated, may hold values from 0 to 1999
- noise: bfloat16 [8192, 512], P('cells'), may hold values from -5 to 5
- emb_weight: bfloat16 [1024, 13500], P(None, 'genes'), may hold values from -0.0546875 to 0.0546875
- ln_gain: float32 [1024], replicated, may hold values from 0.5 to 1.5
- ln_bias: float32 [1024], replicated, may hold values from -1.5 to 1.5
- lat_weight: bfloat16 [1024, 1024], replicated, may hold values from -0.1875 to 0.1875
- lat_bias: float32 [1024], replicated, may hold values from -2 to 2
- up_weight: bfloat16 [1024, 512], replicated, may hold values from -0.25 to 0.25
- dec_weight: bfloat16 [1024, 13500], P(None, 'genes'), may hold values from -0.1875 to 0.1875
- prior_mean: float32 [512, 16], replicated, may hold values from -4 to 4
- prior_logvar: float32 [512, 16], replicated, may hold values from -1 to 1
- out_grad: bfloat16 [8192, 13500], P('cells', 'genes'), may hold values from -6 to 6
Outputs:
- decoded: bfloat16 [8192, 13500], P('cells', 'genes')
- counts_grad: bfloat16 [8192, 13500], P('cells', 'genes')
- emb_weight_grad: float32 [1024, 13500], P('cells', 'genes')
- ln_gain_grad: float32 [1024], P('cells')
- ln_bias_grad: float32 [1024], P('cells')
- lat_weight_grad: float32 [1024, 1024], P('cells')
- lat_bias_grad: float32 [1024], P('cells')
- up_weight_grad: float32 [1024, 512], P('cells')
- dec_weight_grad: float32 [1024, 13500], P('cells', 'genes')
- prior_mean_grad: float32 [512, 16], P('cells')
- prior_logvar_grad: float32 [512, 16], P('cells')
- kl_loss: float32 [1], replicated
Inputs may be any that keep to these rules, and one draw needn't show every extreme that they name: `slide_len`: slide lengths sum to 8192.
All inputs are finite; a program needn't handle non-finite values. No bound on the sum of `cell_mask` on one device may be relied on, other than what follows from the above.
Results may differ from a plain program's by a relative error of at most 0.009.
Values may be sent and summed in bfloat16 or wider, within the bound.
A program may use at most 192 MiB of HBM per device.

v0:
```python
import jax
import jax.numpy as jnp
from jax import lax
from jax.sharding import PartitionSpec as P

WARM = 1000
epsilon = 1e-05
free_bits = 1.0


def exact_dot(left, right):
    return jnp.dot(left, right, precision=lax.Precision.HIGHEST, preferred_element_type=jnp.float32)


def exact_tdot(left, right):
    return lax.dot_general(
        left,
        right,
        (((0,), (0,)), ((), ())),
        precision=lax.Precision.HIGHEST,
        preferred_element_type=jnp.float32,
    )


def half_dot(left, right):
    return jnp.dot(left, right, preferred_element_type=jnp.float32)


def half_tdot(left, right):
    return lax.dot_general(
        left, right, (((0,), (0,)), ((), ())), preferred_element_type=jnp.float32
    )


def half_ntdot(left, right):
    return lax.dot_general(
        left, right, (((1,), (1,)), ((), ())), preferred_element_type=jnp.float32
    )


def bottleneck_forward(
    embedded, noise_rows, ln_gain, ln_bias, lat_weight, lat_bias, up_weight, tables
):
    prec_tab, mean_prec, const_tab = tables
    latent_w = up_weight.shape[1]
    centred = embedded - jnp.mean(embedded, -1, keepdims=True)
    inv_dev = lax.rsqrt(jnp.mean(centred * centred, -1, keepdims=True) + epsilon)
    normal = centred * inv_dev
    hidden = normal * ln_gain + ln_bias
    hidden_low = hidden.astype(jnp.bfloat16)
    latent = half_dot(hidden_low, lat_weight) + lat_bias
    lat_mean = latent[:, :latent_w]
    log_var = latent[:, latent_w:]
    variance = jnp.exp(log_var)
    spread = jnp.exp(0.5 * log_var)
    sample_low = (lat_mean + spread * noise_rows.astype(jnp.float32)).astype(jnp.bfloat16)
    mixed_low = (hidden + half_ntdot(sample_low, up_weight)).astype(jnp.bfloat16)
    logits = -0.5 * (
        exact_dot(lat_mean * lat_mean, prec_tab)
        - 2.0 * exact_dot(lat_mean, mean_prec)
        + jnp.sum(const_tab, 0)
    )
    resp = jax.nn.softmax(logits * latent_w ** (-0.5), axis=-1)
    resp_prec = exact_dot(resp, prec_tab.T)
    resp_mean = exact_dot(resp, mean_prec.T)
    diverge = 0.5 * (
        exact_dot(resp, const_tab.T)
        - log_var
        + (variance + lat_mean * lat_mean) * resp_prec
        - 2.0 * lat_mean * resp_mean
        - 1.0
    )
    kept = (
        normal,
        inv_dev,
        hidden_low,
        lat_mean,
        log_var,
        variance,
        spread,
        sample_low,
        resp,
        resp_prec,
        resp_mean,
    )
    return (mixed_low, diverge, kept)


def bottleneck_backward(
    mixed_grad, weight, noise_rows, kept, ln_gain, lat_weight, up_weight, prior_mean, tables
):
    prec_tab, mean_prec, const_tab = tables
    (
        normal,
        inv_dev,
        hidden_low,
        lat_mean,
        log_var,
        variance,
        spread,
        sample_low,
        resp,
        resp_prec,
        resp_mean,
    ) = kept
    latent_w = up_weight.shape[1]
    up_grad = half_tdot(mixed_grad, sample_low)
    sample_grad = half_dot(mixed_grad, up_weight)
    mean_grad = sample_grad + weight * (lat_mean * resp_prec - resp_mean)
    var_grad = sample_grad * 0.5 * spread * noise_rows.astype(jnp.float32) + 0.5 * weight * (
        variance * resp_prec - 1.0
    )
    moment = variance + lat_mean * lat_mean
    resp_grad = 0.5 * (
        exact_dot(weight, const_tab)
        + exact_dot(weight * moment, prec_tab)
        - 2.0 * exact_dot(weight * lat_mean, mean_prec)
    )
    logit_grad = (
        resp * (resp_grad - jnp.sum(resp * resp_grad, -1, keepdims=True)) * latent_w ** (-0.5)
    )
    mean_grad = (
        mean_grad
        - lat_mean * exact_dot(logit_grad, prec_tab.T)
        + exact_dot(logit_grad, mean_prec.T)
    )
    const_grad = 0.5 * exact_tdot(weight, resp) - 0.5 * jnp.sum(logit_grad, 0)[None, :]
    mprec_grad = -exact_tdot(weight * lat_mean, resp) + exact_tdot(lat_mean, logit_grad)
    prec_grad = (
        0.5 * exact_tdot(weight * moment, resp)
        - 0.5 * exact_tdot(lat_mean * lat_mean, logit_grad)
        + prior_mean * prior_mean * const_grad
        + prior_mean * mprec_grad
    )
    pmean_grad = 2.0 * prior_mean * prec_tab * const_grad + prec_tab * mprec_grad
    plogv_grad = const_grad - prec_tab * prec_grad
    latent_grad = jnp.concatenate([mean_grad, var_grad], axis=1).astype(jnp.bfloat16)
    latb_grad = jnp.sum(latent_grad.astype(jnp.float32), 0)
    latw_grad = half_tdot(hidden_low, latent_grad)
    hidden_grad = mixed_grad.astype(jnp.float32) + half_ntdot(latent_grad, lat_weight)
    gain_grad = jnp.sum(hidden_grad * normal, 0)
    shift_grad = jnp.sum(hidden_grad, 0)
    normal_grad = hidden_grad * ln_gain
    embed_grad = inv_dev * (
        normal_grad
        - jnp.mean(normal_grad, -1, keepdims=True)
        - normal * jnp.mean(normal_grad * normal, -1, keepdims=True)
    )
    small = (latw_grad, up_grad, gain_grad, shift_grad, latb_grad, pmean_grad, plogv_grad)
    return (embed_grad.astype(jnp.bfloat16), small)


def on_device(
    counts,
    library,
    cell_mask,
    slide_len,
    kl_step,
    noise,
    emb_weight,
    ln_gain,
    ln_bias,
    lat_weight,
    lat_bias,
    up_weight,
    dec_weight,
    prior_mean,
    prior_logvar,
    out_grad,
):
    rows = counts.shape[0]
    first = lax.axis_index("cells") * rows
    place = first + jnp.arange(rows, dtype=jnp.int32)
    ends = jnp.cumsum(slide_len)
    slide_of = jnp.sum((ends[None, :] <= place[:, None]).astype(jnp.int32), 1)
    onehot = (slide_of[:, None] == jnp.arange(slide_len.shape[0], dtype=jnp.int32)[None, :]).astype(
        jnp.float32
    )
    live = cell_mask.astype(jnp.float32)
    libsize = library.astype(jnp.float32)
    lib_total, live_total = lax.psum(
        (jnp.sum(onehot * (libsize * live)[:, None], 0), jnp.sum(onehot * live[:, None], 0)),
        "cells",
    )
    slide_lib = lib_total / jnp.maximum(live_total, 1.0)
    scale = jnp.sum(onehot * slide_lib[None, :], 1) / libsize
    total = jnp.maximum(jnp.sum(live_total), 1.0)
    beta = jnp.minimum(1.0, kl_step[0].astype(jnp.float32) / WARM)
    prec_tab = jnp.exp(-prior_logvar)
    tables = (prec_tab, prior_mean * prec_tab, prior_mean * prior_mean * prec_tab + prior_logvar)
    counts_f = counts.astype(jnp.float32)
    normed_low = jnp.log1p(counts_f * scale[:, None]).astype(jnp.bfloat16)
    partial_embed = half_ntdot(normed_low, emb_weight)
    embedded = lax.psum(partial_embed, "genes")
    mixed_low, diverge, kept = bottleneck_forward(
        embedded, noise, ln_gain, ln_bias, lat_weight, lat_bias, up_weight, tables
    )
    kl_sum = lax.psum(jnp.sum(diverge * live[:, None], 0), "cells")
    decoded = half_dot(mixed_low, dec_weight).astype(jnp.bfloat16)
    average = kl_sum / total
    kl_loss = beta * jnp.sum(jnp.maximum(average, free_bits))
    active = (average > free_bits).astype(jnp.float32)
    partial_mixed = half_ntdot(out_grad, dec_weight)
    dec_grad = half_tdot(mixed_low, out_grad)
    weight_rows = beta * active[None, :] * live[:, None] / total
    mixed_grad = lax.psum(partial_mixed, "genes").astype(jnp.bfloat16)
    embed_grad, small = bottleneck_backward(
        mixed_grad, weight_rows, noise, kept, ln_gain, lat_weight, up_weight, prior_mean, tables
    )
    normed_grad = half_dot(embed_grad, emb_weight)
    counts_grad = (normed_grad * scale[:, None] / (1.0 + counts_f * scale[:, None])).astype(
        jnp.bfloat16
    )
    latw_grad, up_grad, gain_grad, shift_grad, latb_grad, pmean_grad, plogv_grad = small
    emb_grad = half_tdot(embed_grad, normed_low)
    summed = (
        lax.psum_scatter(emb_grad, "cells", scatter_dimension=0, tiled=True),
        lax.psum_scatter(dec_grad, "cells", scatter_dimension=0, tiled=True),
        lax.psum_scatter(latw_grad, "cells", scatter_dimension=0, tiled=True),
        lax.psum_scatter(up_grad, "cells", scatter_dimension=0, tiled=True),
        lax.psum_scatter(gain_grad, "cells", scatter_dimension=0, tiled=True),
        lax.psum_scatter(shift_grad, "cells", scatter_dimension=0, tiled=True),
        lax.psum_scatter(latb_grad, "cells", scatter_dimension=0, tiled=True),
        lax.psum_scatter(pmean_grad, "cells", scatter_dimension=0, tiled=True),
        lax.psum_scatter(plogv_grad, "cells", scatter_dimension=0, tiled=True),
    )
    emb_out, dec_out, latw_out, up_out, gain_out, shift_out, latb_out, pmean_out, plogv_out = summed
    return (
        decoded,
        counts_grad,
        emb_out,
        gain_out,
        shift_out,
        latw_out,
        latb_out,
        up_out,
        dec_out,
        pmean_out,
        plogv_out,
        kl_loss.reshape(1),
    )


def solution(mesh):
    placed = (
        P("cells", "genes"),
        P("cells"),
        P("cells"),
        P(),
        P(),
        P("cells", None),
        P(None, "genes"),
        P(),
        P(),
        P(),
        P(),
        P(),
        P(None, "genes"),
        P(),
        P(),
        P("cells", "genes"),
    )
    return jax.shard_map(
        on_device,
        mesh=mesh,
        in_specs=placed,
        out_specs=(
            P("cells", "genes"),
            P("cells", "genes"),
            P("cells", "genes"),
            P("cells"),
            P("cells"),
            P("cells", None),
            P("cells"),
            P("cells", None),
            P("cells", "genes"),
            P("cells", None),
            P("cells", None),
            P(),
        ),
        check_vma=False,
    )
```

profile of v0, /device:TPU:0, one launch (start us, length us, event | category | flops | bytes accessed | tf_op | source)
XLA Modules:
  0.0 957.3 jit_solution(9360086987290301371)
XLA Ops:
  7.2 0.8 convert_element_type.56
  8.8 0.8 reduce-window.8
  9.8 23.1 %all-reduce.4 = (f32[3]{0:T(128)S(1)}, f32[3]{0:T(128)S(1)}) all-reduce(f32[3]{0:T(128)S(1)} %get-tuple-element.17, f32[3]{0:T(128)S(1)} %get-tuple-element.16), channel_id=1, replica_groups=mesh['cells'=8,'genes'=4] {'cells'}, use_global_device_ids=true, to_apply=%region_3.4 | all-reduce | flops 6 | bytes 48 | tf_op jit(solution)/shard_map/psum | solution.py:181
  34.4 14.0 %fusion.1 = f32[1024,1024]{1,0:T(8,128)} fusion(bf16[1024,3375]{0,1:T(8,128)(2,1)} %param.22, bf16[1024,3375]{0,1:T(8,128)(2,1)} %param.16, f32[1024]{0:T(1024)S(1)} %convert_divide_fusion), kind=kOutput, calls=%fused_computation.5 | convolution fusion | flops 7088256000 | bytes 18022400 | tf_op jit(solution)/shard_map/dot_general | solution.py:36
  49.1 14.3 %fusion.64 = f32[1024,1024]{1,0:T(8,128)} fusion(bf16[1024,3375]{0,1:T(8,128)(2,1)} %param.31, bf16[1024,3375]{0,1:T(8,128)(2,1)} %param.28), kind=kOutput, calls=%fused_computation.101 | convolution fusion | flops 7077888000 | bytes 18018304 | tf_op jit(solution)/shard_map/dot_general | solution.py:36
  64.3 67.0 %all-reduce.8.cloned.1.call-done = f32[1024,1024]{1,0:T(8,128)} async-done(((f32[1024,1024]{1,0:T(8,128)}), f32[1024,1024]{1,0:T(8,128)}) %all-reduce.8.cloned.1.call-update) | async-done | bytes 4194320 | tf_op jit(solution)/shard_map/psum | solution.py:194
  131.3 2.4 reduce_sum.166
  133.8 2.9 multiply_reduce_fusion.2
  137.2 2.5 broadcast_add_fusion
  139.7 1.9 convolution_multiply_fusion.1
  141.6 2.0 fusion.63
  143.6 1.8 fusion.55
  145.4 1.9 fusion.41
  147.3 1.3 copy-done.10
  148.6 2.7 multiply_reduce_fusion.4
  151.4 21.8 %psum.39 = f32[512]{0:T(512)S(1)} all-reduce(f32[512]{0:T(512)S(1)} %multiply_reduce_fusion.4), channel_id=1, replica_groups=mesh['cells'=8,'genes'=4] {'cells'}, use_global_device_ids=true, to_apply=%region_15.16 | all-reduce | flops 512 | bytes 4096 | tf_op jit(solution)/shard_map/psum | solution.py:198
  173.7 2.0 fusion.36
  175.8 1.5 convolution_negate_fusion
  177.3 2.3 convolution_add_fusion
  179.6 2.2 multiply_reduce_fusion.5
  181.9 1.4 fusion.26
  183.3 1.3 fusion.23
  184.6 1.2 multiply_add_fusion.1
  185.8 1.7 fusion.31
  187.5 0.8 copy.45
  188.5 76.6 %all-reduce.9 = bf16[1024,1024]{1,0:T(8,128)(2,1)} all-reduce(f32[1024,1024]{1,0:T(8,128)} %fusion.64), channel_id=1, replica_groups=mesh['cells'=8,'genes'=4] {'genes'}, use_global_device_ids=true, to_apply=%region_10.11 | all-reduce | flops 1048576 | bytes 6291456 | tf_op jit(solution)/shard_map/psum | solution.py:206
  265.1 0.8 copy.43
  266.0 7.7 fusion.6
  273.7 1.0 copy-done.20
  274.7 2.7 fusion.66
  277.5 1.8 fusion.40
  279.3 6.0 add_convert_fusion.1
  285.4 1.0 copy-done.11
  286.4 4.5 fusion.37
  291.2 8.4 multiply_reduce_fusion
  299.5 19.0 %fusion = f32[1024,3375]{0,1:T(8,128)} fusion(bf16[1024,3375]{0,1:T(8,128)(2,1)} %param.16, f32[1024]{0:T(1024)S(1)} %convert_divide_fusion, f32[1024,1024]{1,0:T(8,128)} %get-tuple-element.40, f32[1024,1024]{1,0:T(8,128)S(1)} %copy-done.4, f32[1024]{0:T(1024)S(1)} %get-tuple-element.43, f32[1024]{0:T(1024)S(1)} %get-tuple-element.44, ...), kind=kOutput, calls=%fused_computation.4 | convolution fusion | flops 7096644608 | bytes 29149184 | tf_op jit(solution)/shard_map/dot_general | solution.py:30
  318.9 0.9 copy-done.15
  320.1 3.6 add_convert_fusion
  323.7 1.3 copy-done.22
  325.0 13.4 %fusion.65 = f32[1024,3375]{0,1:T(8,128)} fusion(bf16[1024,1024]{1,0:T(8,128)(2,1)S(1)} %add_convert_fusion, bf16[1024,3375]{0,1:T(8,128)(2,1)} %param.31), kind=kOutput, calls=%fused_computation.102 | convolution fusion | flops 7077888000 | bytes 22833152 | tf_op jit(solution)/shard_map/dot_general | solution.py:30
  340.7 33.7 %all-reduce.3 = (f32[1024]{0:T(1024)S(1)}, f32[1024]{0:T(1024)S(1)}, f32[1024]{0:T(1024)S(1)}) all-reduce(f32[1024]{0:T(1024)S(1)} %get-tuple-element.12, f32[1024]{0:T(1024)S(1)} %get-tuple-element.15, f32[1024]{0:T(1024)S(1)} %convert_reduce_fusion), channel_id=3, replica_groups=mesh['cells'=8,'genes'=4] {'cells'}, use_global_device_ids=true, to_apply=%region_22.23.clone | all-reduce | flops 3072 | bytes 24576
  376.8 12.2 %convolution_convert_fusion = bf16[1024,3375]{0,1:T(8,128)(2,1)} fusion(bf16[1024,1024]{1,0:T(8,128)(2,1)} %copy-done.22, bf16[1024,3375]{0,1:T(8,128)(2,1)} %param.28), kind=kOutput, calls=%fused_computation.3 | convolution fusion | flops 7081344000 | bytes 15921152 | tf_op jit(solution)/shard_map/dot_general | solution.py:26
  389.0 16.2 %divide_convert_fusion = bf16[1024,3375]{0,1:T(8,128)(2,1)} fusion(bf16[1024,3375]{0,1:T(8,128)(2,1)} %param.16, bf16[1024,3375]{0,1:T(8,128)(2,1)} %param.22, f32[1024]{0:T(1024)S(1)} %convert_divide_fusion, f32[1024,1024]{1,0:T(8,128)S(1)} %copy-done.23, f32[1024,1024]{1,0:T(8,128)S(1)} %copy-done.5, f32[1024]{0:T(1024)S(1)} %get-tuple-element.43, ...), kind=kOutput, calls=%fused_computation | convolution fusion | flops 7107012608 | bytes 29149184 | tf_op jit(solution)/shard_map/dot_general | solution.py:26
  405.2 1.4 copy.46
  406.6 1.4 copy.44
  408.0 79.9 %reduce-scatter.13.cloned.1.call-done = f32[128,1024]{1,0:T(8,128)} async-done(((f32[1024,1024]{1,0:T(8,128)}), f32[128,1024]{1,0:T(8,128)}) %reduce-scatter.13.cloned.1.call-update) | async-done | bytes 524304 | tf_op jit(solution)/shard_map/reduce_scatter | solution.py:219
  487.9 230.7 %reduce-scatter.11.cloned.1.call-done = f32[128,3375]{0,1:T(8,128)} async-done(((f32[1024,3375]{0,1:T(8,128)}), f32[128,3375]{0,1:T(8,128)}) %reduce-scatter.11.cloned.1.call-update) | async-done | bytes 1728016 | tf_op jit(solution)/shard_map/reduce_scatter | solution.py:217
  718.6 230.2 %reduce-scatter.17.cloned.1.call-done = f32[128,3375]{0,1:T(8,128)} async-done(((f32[1024,3375]{0,1:T(8,128)}), f32[128,3375]{0,1:T(8,128)}) %reduce-scatter.17.cloned.1.call-update) | async-done | bytes 1728016 | tf_op jit(solution)/shard_map/reduce_scatter | solution.py:218
  (80 shorter events, 8.3 us)
Async XLA Ops:
  7.2 129.5 %copy-start = (bf16[1024,1024]{1,0:T(8,128)(2,1)S(1)}, bf16[1024,1024]{1,0:T(8,128)(2,1)}, u32[]{:S(2)}) copy-start(bf16[1024,1024]{1,0:T(8,128)(2,1)} %param.25) | copy-start | bytes 6291460
  7.2 124.1 %all-reduce.8.cloned.1.call-start = ((), (), s32[]{:S(2)}) async-start(), calls=%async_computation.6 | async-start | bytes 8388608 | tf_op jit(solution)/shard_map/psum | solution.py:194
  48.4 356.8 %reduce-scatter.21.cloned.1.call-start = ((), (), s32[]{:S(2)}) async-start(), calls=%async_computation.12 | async-start | bytes 294912
  49.1 15.0 %copy-start.13 = (f32[512,16]{0,1:T(8,128)S(1)}, f32[512,16]{0,1:T(8,128)}, u32[]{:S(2)}) copy-start(f32[512,16]{0,1:T(8,128)} %param.30) | copy-start | bytes 98308
  49.1 15.0 %copy-start.14 = (f32[512,16]{0,1:T(8,128)S(1)}, f32[512,16]{0,1:T(8,128)}, u32[]{:S(2)}) copy-start(f32[512,16]{0,1:T(8,128)} %param.29) | copy-start | bytes 98308
  64.3 72.5 %copy-start.16 = (f32[1024]{0:T(1024)S(1)}, f32[1024]{0:T(1024)}, u32[]{:S(2)}) copy-start(f32[1024]{0:T(1024)} %param.26) | copy-start | bytes 12292
  64.3 72.5 %copy-start.17 = (f32[1024]{0:T(1024)S(1)}, f32[1024]{0:T(1024)}, u32[]{:S(2)}) copy-start(f32[1024]{0:T(1024)} %param.24) | copy-start | bytes 12292
  64.3 72.5 %copy-start.18 = (f32[1024]{0:T(1024)S(1)}, f32[1024]{0:T(1024)}, u32[]{:S(2)}) copy-start(f32[1024]{0:T(1024)} %param.23) | copy-start | bytes 12292
  133.8 3.5 copy-start.2
  139.7 7.6 copy-start.6
  145.4 1.9 copy-start.9
  147.3 1.3 copy-start.10
  173.1 2.7 copy-start.7
  188.4 218.2 %reduce-scatter.19.cloned.1.call-start = ((), (), s32[]{:S(2)}) async-start(), calls=%async_computation.11 | async-start | bytes 294912
  265.9 142.1 %reduce-scatter.15.cloned.1.call-start = ((), (), s32[]{:S(2)}) async-start(), calls=%async_computation.9 | async-start | bytes 2359296 | tf_op jit(solution)/shard_map/reduce_scatter | solution.py:220
  266.0 8.7 copy-start.8
  273.7 1.0 copy-start.20
  277.4 210.5 %reduce-scatter.13.cloned.1.call-start = ((), (), s32[]{:S(2)}) async-start(), calls=%async_computation.8 | async-start | bytes 4718592 | tf_op jit(solution)/shard_map/reduce_scatter | solution.py:219
  279.3 7.0 copy-start.3
  285.4 1.0 copy-start.11
  290.9 427.7 %reduce-scatter.11.cloned.1.call-start = ((), (), s32[]{:S(2)}) async-start(), calls=%async_computation.7 | async-start | bytes 15556608 | tf_op jit(solution)/shard_map/reduce_scatter | solution.py:217
  291.2 8.4 copy-start.4
  318.5 1.2 copy-start.15
  318.5 1.5 copy-start.21
  318.6 630.3 %reduce-scatter.17.cloned.1.call-start = ((), (), s32[]{:S(2)}) async-start(), calls=%async_computation.10 | async-start | bytes 15556608 | tf_op jit(solution)/shard_map/reduce_scatter | solution.py:218
  323.7 1.3 copy-start.22
  338.4 0.7 copy-start.19
  338.4 1.9 copy-start.12
  376.8 12.2 %copy-start.5 = (f32[1024,1024]{1,0:T(8,128)S(1)}, f32[1024,1024]{1,0:T(8,128)}, u32[]{:S(2)}) copy-start(f32[1024,1024]{1,0:T(8,128)} %all-reduce.8.cloned.1.call-done) | copy-start | bytes 12582916
  376.8 12.2 %copy-start.23 = (f32[1024,1024]{1,0:T(8,128)S(1)}, f32[1024,1024]{1,0:T(8,128)}, u32[]{:S(2)}) copy-start(f32[1024,1024]{1,0:T(8,128)} %get-tuple-element.40) | copy-start | bytes 12582916
  389.0 559.8 %copy-start.1 = (bf16[1024,1024]{1,0:T(8,128)(2,1)S(1)}, bf16[1024,1024]{1,0:T(8,128)(2,1)}, u32[]{:S(2)}) copy-start(bf16[1024,1024]{1,0:T(8,128)(2,1)} %param.25) | copy-start | bytes 6291460
Sparse Core Ops, SparseCore 0:
  48.5 82.7 all-reduce.7
  188.5 58.4 reduce-scatter.20
  266.1 58.3 reduce-scatter.18
  328.4 68.1 reduce-scatter.14
  400.6 87.2 reduce-scatter.12
  491.9 226.6 reduce-scatter.10
  722.7 226.0 reduce-scatter.16
where the time goes:
time: 963 us; the launch traced here: 957 us
  waiting for transfers between devices  608 us (63%)
  blocking collectives  155 us (16%)
  matrix products  150 us (16%)
  between operations  18.7 us (2%)
  local copies, waits for them, and re-layouts  13.8 us (1%)
  other arithmetic  10.6 us (1%)
    reduce_scatter x1, waiting for transfers between devices, on_device(): lax.psum_scatter(emb_grad, 'cells', scatter_dimension=0, tiled=True)  231 us
    reduce_scatter x1, waiting for transfers between devices, on_device(): lax.psum_scatter(dec_grad, 'cells', scatter_dimension=0, tiled=True)  230 us
    reduce_scatter x1, waiting for transfers between devices, on_device(): lax.psum_scatter(latw_grad, 'cells', scatter_dimension=0, tiled=True)  79.9 us
    psum x1, blocking collectives, on_device(): mixed_grad = lax.psum(partial_mixed, 'genes').astype(jnp.bfloat16)  76.6 us
    psum x1, waiting for transfers between devices, on_device(): embedded = lax.psum(partial_embed, 'genes')  67 us
    dot_general x4, matrix products, half_ntdot(): lax.dot_general(left, right, (((1,), (1,)), ((), ())), preferred_element_...  40.3 us
    dot_general x4, matrix products, half_tdot(): lax.dot_general(left, right, (((0,), (0,)), ((), ())), preferred_element_...  39.6 us
    dot_general x4, matrix products, half_dot(): return jnp.dot(left, right, preferred_element_type=jnp.float32)  38.5 us
  transfers between devices with their start and end apart: 7, of which 4 were waited for; matrix products, arithmetic and copies ran while one was open for 12% of the time, Pallas kernels for 0%

commit v1 on v0

--- a/solution.py
+++ b/solution.py
@@ -1,3 +1,4 @@
+import functools
 import jax
 import jax.numpy as jnp
 from jax import lax
@@ -6,6 +7,14 @@
 WARM = 1000
 epsilon = 1e-05
 free_bits = 1.0
+
+
+def view_the_ranges(slab_in, which_axis):
+    w_next = lax.all_gather(slab_in, which_axis).sum(axis=0)
+    return w_next
+
+
+convert_object = functools.partial(view_the_ranges, which_axis="genes")
 
 
 def exact_dot(left, right):
@@ -191,7 +200,7 @@
     counts_f = counts.astype(jnp.float32)
     normed_low = jnp.log1p(counts_f * scale[:, None]).astype(jnp.bfloat16)
     partial_embed = half_ntdot(normed_low, emb_weight)
-    embedded = lax.psum(partial_embed, "genes")
+    embedded = convert_object(partial_embed)
     mixed_low, diverge, kept = bottleneck_forward(
         embedded, noise, ln_gain, ln_bias, lat_weight, lat_bias, up_weight, tables
     )

time: 963 us -> 998 us (1.036)
  waiting for transfers between devices: 608 us -> 628 us
  other arithmetic: 10.6 us -> 25.1 us
    all_gather x0 -> x1, waiting for transfers between devices: none -> 87.5 us  [view_the_ranges(): w_next = lax.all_gather(slab_in, which_axis).sum(axis=0)]
    psum x1 -> x0, waiting for transfers between devices: 67 us -> none  [on_device(): embedded = lax.psum(partial_embed, 'genes')]
    reduce_sum x0 -> x1, other arithmetic: none -> 10.4 us  [view_the_ranges(): w_next = lax.all_gather(slab_in, which_axis).sum(axis=0)]
where the time goes in v1:
time: 998 us; the launch traced here: 992 us
  waiting for transfers between devices  628 us (63%)
  blocking collectives  155 us (16%)
  matrix products  151 us (15%)
  other arithmetic  25.1 us (3%)
  between operations  18.8 us (2%)
  local copies, waits for them, and re-layouts  13.8 us (1%)
    reduce_scatter x1, waiting for transfers between devices, on_device(): lax.psum_scatter(emb_grad, 'cells', scatter_dimension=0, tiled=True)  231 us
    reduce_scatter x1, waiting for transfers between devices, on_device(): lax.psum_scatter(dec_grad, 'cells', scatter_dimension=0, tiled=True)  230 us
    all_gather x1, waiting for transfers between devices, view_the_ranges(): w_next = lax.all_gather(slab_in, which_axis).sum(axis=0)  87.5 us
    reduce_scatter x1, waiting for transfers between devices, on_device(): lax.psum_scatter(latw_grad, 'cells', scatter_dimension=0, tiled=True)  79.5 us
    psum x1, blocking collectives, on_device(): mixed_grad = lax.psum(partial_mixed, 'genes').astype(jnp.bfloat16)  76.8 us
    dot_general x4, matrix products, half_ntdot(): lax.dot_general(left, right, (((1,), (1,)), ((), ())), preferred_element_...  40.2 us
    dot_general x4, matrix products, half_tdot(): lax.dot_general(left, right, (((0,), (0,)), ((), ())), preferred_element_...  39.8 us
    dot_general x4, matrix products, half_dot(): return jnp.dot(left, right, preferred_element_type=jnp.float32)  38.5 us
  transfers between devices with their start and end apart: 7, of which 4 were waited for; matrix products, arithmetic and copies ran while one was open for 12% of the time, Pallas kernels for 0%

profile of v1, /device:TPU:0, one launch (start us, length us, event | category | flops | bytes accessed | tf_op | source)
XLA Modules:
  0.0 992.1 jit_solution(17668735077179433084)
XLA Ops:
  7.2 0.8 convert_element_type.56
  9.8 23.1 %all-reduce.4 = (f32[3]{0:T(128)S(1)}, f32[3]{0:T(128)S(1)}) all-reduce(f32[3]{0:T(128)S(1)} %get-tuple-element.17, f32[3]{0:T(128)S(1)} %get-tuple-element.16), channel_id=1, replica_groups=mesh['cells'=8,'genes'=4] {'cells'}, use_global_device_ids=true, to_apply=%region_3.4 | all-reduce | flops 6 | bytes 48 | tf_op jit(solution)/shard_map/psum | solution.py:190
  34.4 14.0 %fusion.1 = f32[1024,1024]{1,0:T(8,128)} fusion(bf16[1024,3375]{0,1:T(8,128)(2,1)} %param.22, bf16[1024,3375]{0,1:T(8,128)(2,1)} %param.16, f32[1024]{0:T(1024)S(1)} %convert_divide_fusion), kind=kOutput, calls=%fused_computation.5 | convolution fusion | flops 7088256000 | bytes 18022400 | tf_op jit(solution)/shard_map/dot_general | solution.py:45
  49.1 14.3 %fusion.64 = f32[1024,1024]{1,0:T(8,128)} fusion(bf16[1024,3375]{0,1:T(8,128)(2,1)} %param.31, bf16[1024,3375]{0,1:T(8,128)(2,1)} %param.28), kind=kOutput, calls=%fused_computation.101 | convolution fusion | flops 7077888000 | bytes 18018304 | tf_op jit(solution)/shard_map/dot_general | solution.py:45
  64.3 87.5 %all-gather.3.cloned.1.call-done = f32[4096,1024]{1,0:T(8,128)} async-done(((f32[1024,1024]{1,0:T(8,128)}), f32[4096,1024]{1,0:T(8,128)}) %all-gather.3.cloned.1.call-update) | async-done | bytes 16777232 | tf_op jit(solution)/shard_map/all_gather | solution.py:13
  151.8 10.4 %reduce_sum.175 = f32[1024,1024]{1,0:T(8,128)} reduce(f32[4,1024,1024]{2,1,0:T(8,128)} %bitcast.32, f32[]{:T(128)} %constant.22.clone.1), dimensions={0}, to_apply=%region_7.8 | reduce | flops 3145728 | bytes 20971524 | tf_op jit(solution)/shard_map/reduce_sum | solution.py:13
  162.1 6.6 reduce.1
  168.8 2.9 multiply_reduce_fusion.2
  172.2 2.5 broadcast_add_fusion
  174.7 1.9 convolution_multiply_fusion.1
  176.6 2.0 fusion.63
  178.6 1.8 fusion.55
  180.4 1.9 fusion.41
  182.3 1.3 copy-done.10
  183.6 3.2 multiply_reduce_fusion.4
  186.8 21.4 %psum.31 = f32[512]{0:T(512)S(1)} all-reduce(f32[512]{0:T(512)S(1)} %multiply_reduce_fusion.4), channel_id=1, replica_groups=mesh['cells'=8,'genes'=4] {'cells'}, use_global_device_ids=true, to_apply=%region_15.16 | all-reduce | flops 512 | bytes 4096 | tf_op jit(solution)/shard_map/psum | solution.py:207
  208.8 2.0 fusion.36
  210.8 1.5 convolution_negate_fusion
  212.3 2.3 convolution_add_fusion
  214.7 2.2 multiply_reduce_fusion.5
  217.0 1.4 fusion.26
  218.4 1.3 fusion.23
  219.6 1.2 multiply_add_fusion.1
  220.9 1.7 fusion.31
  222.6 0.8 copy.45
  223.5 76.8 %all-reduce.6 = bf16[1024,1024]{1,0:T(8,128)(2,1)} all-reduce(f32[1024,1024]{1,0:T(8,128)} %fusion.64), channel_id=1, replica_groups=mesh['cells'=8,'genes'=4] {'genes'}, use_global_device_ids=true, to_apply=%region_10.11 | all-reduce | flops 1048576 | bytes 6291456 | tf_op jit(solution)/shard_map/psum | solution.py:215
  300.3 0.8 copy.43
  301.2 7.7 fusion.6
  308.9 1.0 copy-done.20
  309.9 2.7 fusion.66
  312.7 1.8 fusion.40
  314.5 6.0 add_convert_fusion.1
  320.6 1.0 copy-done.11
  321.5 4.7 fusion.37
  326.5 8.3 multiply_reduce_fusion
  334.8 19.0 %fusion = f32[1024,3375]{0,1:T(8,128)} fusion(bf16[1024,3375]{0,1:T(8,128)(2,1)} %param.16, f32[1024]{0:T(1024)S(1)} %convert_divide_fusion, f32[1024,1024]{1,0:T(8,128)} %get-tuple-element.40, f32[1024,1024]{1,0:T(8,128)S(1)} %copy-done.6, f32[1024]{0:T(1024)S(1)} %get-tuple-element.43, f32[1024]{0:T(1024)S(1)} %get-tuple-element.44, ...), kind=kOutput, calls=%fused_computation.4 | convolution fusion | flops 7096644608 | bytes 29149184 | tf_op jit(solution)/shard_map/dot_general | solution.py:39
  354.1 0.9 copy-done.15
  355.4 3.6 add_convert_fusion
  359.0 1.3 copy-done.22
  360.3 13.4 %fusion.65 = f32[1024,3375]{0,1:T(8,128)} fusion(bf16[1024,1024]{1,0:T(8,128)(2,1)S(1)} %add_convert_fusion, bf16[1024,3375]{0,1:T(8,128)(2,1)} %param.31), kind=kOutput, calls=%fused_computation.102 | convolution fusion | flops 7077888000 | bytes 22833152 | tf_op jit(solution)/shard_map/dot_general | solution.py:39
  376.0 33.6 %all-reduce.3 = (f32[1024]{0:T(1024)S(1)}, f32[1024]{0:T(1024)S(1)}, f32[1024]{0:T(1024)S(1)}) all-reduce(f32[1024]{0:T(1024)S(1)} %get-tuple-element.12, f32[1024]{0:T(1024)S(1)} %get-tuple-element.15, f32[1024]{0:T(1024)S(1)} %convert_reduce_fusion), channel_id=4, replica_groups=mesh['cells'=8,'genes'=4] {'cells'}, use_global_device_ids=true, to_apply=%region_22.23.clone | all-reduce | flops 3072 | bytes 24576
  412.0 12.2 %convolution_convert_fusion = bf16[1024,3375]{0,1:T(8,128)(2,1)} fusion(bf16[1024,1024]{1,0:T(8,128)(2,1)} %copy-done.22, bf16[1024,3375]{0,1:T(8,128)(2,1)} %param.28), kind=kOutput, calls=%fused_computation.3 | convolution fusion | flops 7081344000 | bytes 15921152 | tf_op jit(solution)/shard_map/dot_general | solution.py:35
  424.2 16.2 %divide_convert_fusion = bf16[1024,3375]{0,1:T(8,128)(2,1)} fusion(bf16[1024,3375]{0,1:T(8,128)(2,1)} %param.16, bf16[1024,3375]{0,1:T(8,128)(2,1)} %param.22, f32[1024]{0:T(1024)S(1)} %convert_divide_fusion, f32[1024,1024]{1,0:T(8,128)S(1)} %copy-done.23, f32[1024,1024]{1,0:T(8,128)S(1)} %copy-done.7, f32[1024]{0:T(1024)S(1)} %get-tuple-element.43, ...), kind=kOutput, calls=%fused_computation | convolution fusion | flops 7107012608 | bytes 29149184 | tf_op jit(solution)/shard_map/dot_general | solution.py:35
  440.4 1.4 copy.46
  441.8 1.4 copy.44
  443.2 79.5 %reduce-scatter.13.cloned.1.call-done = f32[128,1024]{1,0:T(8,128)} async-done(((f32[1024,1024]{1,0:T(8,128)}), f32[128,1024]{1,0:T(8,128)}) %reduce-scatter.13.cloned.1.call-update) | async-done | bytes 524304 | tf_op jit(solution)/shard_map/reduce_scatter | solution.py:228
  522.7 230.7 %reduce-scatter.11.cloned.1.call-done = f32[128,3375]{0,1:T(8,128)} async-done(((f32[1024,3375]{0,1:T(8,128)}), f32[128,3375]{0,1:T(8,128)}) %reduce-scatter.11.cloned.1.call-update) | async-done | bytes 1728016 | tf_op jit(solution)/shard_map/reduce_scatter | solution.py:226
  753.4 230.2 %reduce-scatter.17.cloned.1.call-done = f32[128,3375]{0,1:T(8,128)} async-done(((f32[1024,3375]{0,1:T(8,128)}), f32[128,3375]{0,1:T(8,128)}) %reduce-scatter.17.cloned.1.call-update) | async-done | bytes 1728016 | tf_op jit(solution)/shard_map/reduce_scatter | solution.py:227
  (83 shorter events, 9.2 us)
Async XLA Ops:
  7.2 164.5 %copy-start = (bf16[1024,1024]{1,0:T(8,128)(2,1)S(1)}, bf16[1024,1024]{1,0:T(8,128)(2,1)}, u32[]{:S(2)}) copy-start(bf16[1024,1024]{1,0:T(8,128)(2,1)} %param.25) | copy-start | bytes 6291460
  7.2 144.6 %all-gather.3.cloned.1.call-start = ((), (), s32[]{:S(2)}) async-start(), calls=%async_computation.10 | async-start | bytes 20971520 | tf_op jit(solution)/shard_map/all_gather | solution.py:13
  48.4 392.0 %reduce-scatter.21.cloned.1.call-start = ((), (), s32[]{:S(2)}) async-start(), calls=%async_computation.12 | async-start | bytes 294912
  49.1 15.0 %copy-start.13 = (f32[512,16]{0,1:T(8,128)S(1)}, f32[512,16]{0,1:T(8,128)}, u32[]{:S(2)}) copy-start(f32[512,16]{0,1:T(8,128)} %param.30) | copy-start | bytes 98308
  49.1 15.0 %copy-start.14 = (f32[512,16]{0,1:T(8,128)S(1)}, f32[512,16]{0,1:T(8,128)}, u32[]{:S(2)}) copy-start(f32[512,16]{0,1:T(8,128)} %param.29) | copy-start | bytes 98308
  168.7 3.0 copy-start.16
  168.7 3.0 copy-start.17
  168.7 3.0 copy-start.18
  168.8 3.5 copy-start.4
  174.7 7.6 copy-start.2
  180.4 1.9 copy-start.9
  182.3 1.3 copy-start.10
  208.2 2.7 copy-start.3
  223.4 218.4 %reduce-scatter.19.cloned.1.call-start = ((), (), s32[]{:S(2)}) async-start(), calls=%async_computation.11 | async-start | bytes 294912
  301.2 142.1 %reduce-scatter.15.cloned.1.call-start = ((), (), s32[]{:S(2)}) async-start(), calls=%async_computation.8 | async-start | bytes 2359296 | tf_op jit(solution)/shard_map/reduce_scatter | solution.py:229
  301.2 8.7 copy-start.8
  308.9 1.0 copy-start.20
  312.6 210.1 %reduce-scatter.13.cloned.1.call-start = ((), (), s32[]{:S(2)}) async-start(), calls=%async_computation.7 | async-start | bytes 4718592 | tf_op jit(solution)/shard_map/reduce_scatter | solution.py:228
  314.5 7.0 copy-start.5
  320.6 1.0 copy-start.11
  326.3 427.1 %reduce-scatter.11.cloned.1.call-start = ((), (), s32[]{:S(2)}) async-start(), calls=%async_computation.6 | async-start | bytes 15556608 | tf_op jit(solution)/shard_map/reduce_scatter | solution.py:226
  326.5 8.3 copy-start.6
  353.8 1.2 copy-start.15
  353.8 1.5 copy-start.21
  353.8 629.8 %reduce-scatter.17.cloned.1.call-start = ((), (), s32[]{:S(2)}) async-start(), calls=%async_computation.9 | async-start | bytes 15556608 | tf_op jit(solution)/shard_map/reduce_scatter | solution.py:227
  359.0 1.3 copy-start.22
  373.7 0.7 copy-start.19
  373.7 1.9 copy-start.12
  412.0 12.2 %copy-start.7 = (f32[1024,1024]{1,0:T(8,128)S(1)}, f32[1024,1024]{1,0:T(8,128)}, u32[]{:S(2)}) copy-start(f32[1024,1024]{1,0:T(8,128)} %reduce_sum.175) | copy-start | bytes 12582916
  412.0 12.2 %copy-start.23 = (f32[1024,1024]{1,0:T(8,128)S(1)}, f32[1024,1024]{1,0:T(8,128)}, u32[]{:S(2)}) copy-start(f32[1024,1024]{1,0:T(8,128)} %get-tuple-element.40) | copy-start | bytes 12582916
  424.2 559.4 %copy-start.1 = (bf16[1024,1024]{1,0:T(8,128)(2,1)S(1)}, bf16[1024,1024]{1,0:T(8,128)(2,1)}, u32[]{:S(2)}) copy-start(bf16[1024,1024]{1,0:T(8,128)(2,1)} %param.25) | copy-start | bytes 6291460
Sparse Core Ops, SparseCore 0:
  48.5 103.1 all-gather.2
  223.6 58.3 reduce-scatter.20
  301.3 58.2 reduce-scatter.18
  363.5 67.6 reduce-scatter.14
  435.3 87.3 reduce-scatter.12
  526.6 226.6 reduce-scatter.10
  757.5 226.0 reduce-scatter.16
